TPU v7x, 32 devices: a whole 2x2x4 slice. The times are simulated.
32 devices in a mesh: groups: 2 (over y), rank: 16 (over z, x, core).
Axes of the slice: x: 2, y: 2, z: 4, core: 2. Of those that a mesh axis runs over, the one named last changes fastest.
Arguments:
- pool: bfloat16 [512, 1024], P(('groups', 'rank')), parts along dimension 0, may hold values from -6 to 6
- kv_cache: bfloat16 [128, 4, 64, 256], P(('groups', 'rank')), parts along dimension 0
- w_qu: bfloat16 [1024, 1024], replicated, may hold values from -0.1875 to 0.1875
- w_out: bfloat16 [512, 1024], replicated, may hold values from -0.25 to 0.25
- norm_gain: float32 [512], replicated, may hold values from 0.1 to 1.9
- cand_ids: int32 [8, 2048], P('groups'), parts along dimension 0, may hold values from 0 to 255
- ranker: int32 [4], replicated, may hold values from 0 to 3, each once
- hist_blocks: int32 [8], P('groups'), parts along dimension 0, may hold values from 4 to 16, as said below
- cache_slot: int32 [8, 16], P('groups'), parts along dimension 0, may hold values from 0 to 63, as said below
Outputs:
- ranked: bfloat16 [16384, 1024], P(('groups', 'rank')), parts along dimension 0
There are 2 independent parts, one for each index of `groups`. A program takes and returns all parts, laid end to end along the dimension named above; an argument that names none is the same for every part. Nothing has to cross between parts.
Inputs may be any that keep to these rules, and one draw needn't show every extreme that they name: Block b of user u (b < 16) is held in slot cache_slot[u, b], which lies on device cache_slot[u, b] // 4 of the rank axis. Each slot holds exactly one pair (u, b); the 16 blocks of one user lie on 16 different devices. `ranker`: each ranking group scores exactly one user. User u's history is its blocks 0 to hist_blocks[u] - 1; its other blocks are unused. Some user has 16 blocks.
All inputs are finite; a program needn't handle non-finite values.
Results may differ from a plain program's by a relative error of at most 0.0054.
Values may be sent and summed in bfloat16 or wider, within the bound.
No kernel may reach another device: no remote copies, remote signals or barrier semaphores. Data moves between devices by JAX's collectives and lax.ppermute only.
A program may use at most 128 MiB of HBM per device.

v0:
```python
import math
import jax
import jax.numpy as jnp
from jax import lax
from jax.sharding import PartitionSpec as P

norm_eps = 1e-05


def partner(shard, axis, bit):
    return lax.ppermute(shard, axis, [(i, i ^ 1 << bit) for i in range(lax.axis_size(axis))])


def attend_blocks(queries, stacked, head_dim, live_steps):
    score_scale = 1.0 / math.sqrt(head_dim)

    def step_fn(running, item):
        step_index, key_block = item

        def compute(total):
            key_part = key_block[:, :head_dim]
            value_part = key_block[:, head_dim:]
            scores = lax.dot_general(
                queries, key_part, (((1,), (1,)), ((), ())), preferred_element_type=jnp.float32
            )
            weights = jax.nn.silu(scores * score_scale).astype(jnp.bfloat16)
            return total + jnp.dot(weights, value_part, preferred_element_type=jnp.float32)

        def keep_same(total):
            return total

        return (lax.cond(step_index < live_steps, compute, keep_same, running), None)

    initial = jnp.zeros((queries.shape[0], head_dim), jnp.float32)
    step_ids = jnp.arange(stacked.shape[0], dtype=jnp.int32)
    attended, unused = lax.scan(step_fn, initial, (step_ids, stacked))
    return attended


def body(pool, kv_cache, w_qu, w_out, norm_gain, cand_ids, ranker, hist_blocks, cache_slot):
    devices = lax.axis_size("rank")
    my_index = lax.axis_index("rank")
    slots_here, head_count, block_len, pair_width = kv_cache.shape
    head_dim = pair_width // 2
    user_count, most_blocks = cache_slot.shape
    model_width = pool.shape[1]
    cand_count = cand_ids.shape[1]
    slice_width = model_width // head_count
    qu_cols = 2 * head_dim
    my_group = my_index // head_count
    my_head = my_index % head_count
    bit_count = head_count.bit_length() - 1
    share_rows = cand_count // head_count
    user_range = jnp.arange(user_count, dtype=jnp.int32)
    group_match = ranker[None, :] == user_range[:, None]
    user_of_group = jnp.sum(jnp.where(group_match, user_range[None, :], 0), axis=1)
    my_user = jnp.sum(jnp.where(user_range == my_group, user_of_group, 0))
    block_range = jnp.arange(most_blocks, dtype=jnp.int32)
    live_blocks = block_range[None, :] < hist_blocks[:, None]
    owner_table = cache_slot // slots_here
    held_here = live_blocks & (owner_table == my_index)
    held_slot = jnp.sum(jnp.where(held_here, cache_slot % slots_here, 0), axis=1)
    held_flag = jnp.any(held_here, axis=1)
    slot_of_group = jnp.sum(jnp.where(group_match, held_slot[None, :], 0), axis=1)
    flag_of_group = jnp.any(group_match & held_flag[None, :], axis=1)
    outgoing = jnp.take(kv_cache, slot_of_group, axis=0)
    outgoing = jnp.where(flag_of_group[:, None, None, None], outgoing, jnp.zeros_like(outgoing))
    outgoing = outgoing.reshape(devices, block_len, pair_width)
    incoming = lax.all_to_all(outgoing, "rank", split_axis=0, concat_axis=0, tiled=True)
    my_ids = lax.dynamic_index_in_dim(cand_ids, my_user, 0, keepdims=False)
    whole_pool = lax.all_gather(pool, "rank", axis=0, tiled=True)
    cand_rows = jnp.take(whole_pool, my_ids, axis=0)
    w_head = lax.dynamic_slice_in_dim(w_qu, my_head * qu_cols, qu_cols, 1)
    head_qu = jax.nn.silu(jnp.dot(cand_rows, w_head, preferred_element_type=jnp.float32)).astype(
        jnp.bfloat16
    )
    x_part = lax.dynamic_slice_in_dim(cand_rows, my_head * slice_width, slice_width, 1)
    queries = head_qu[:, :head_dim]
    gate_part = head_qu[:, head_dim:]
    step_sources = min(16, devices)
    stacked = incoming.reshape(devices // step_sources, step_sources * block_len, pair_width)
    live_steps = stacked.shape[0]
    attended = attend_blocks(queries, stacked, head_dim, live_steps)
    total_width = head_count * head_dim
    carried = jnp.concatenate(
        [attended, gate_part.astype(jnp.float32), x_part.astype(jnp.float32)], axis=1
    )
    state = carried.reshape(head_count, share_rows, 1, carried.shape[1])
    for bit_index in reversed(range(bit_count)):
        half_count = state.shape[0] // 2
        lower_half = state[:half_count]
        upper_half = state[half_count:]
        upper_side = my_head >> bit_index & 1 == 1
        keeping = jnp.where(upper_side, upper_half, lower_half)
        giving = jnp.where(upper_side, lower_half, upper_half)
        received = partner(giving, "rank", bit_index)
        state = jnp.where(
            upper_side,
            jnp.concatenate([received, keeping], axis=2),
            jnp.concatenate([keeping, received], axis=2),
        )
    reversal = [
        sum(((source >> bit & 1) << bit_count - 1 - bit for bit in range(bit_count)))
        for source in range(head_count)
    ]
    ordered = state[0][:, jnp.array(reversal, dtype=jnp.int32), :]
    att_rows = ordered[:, :, :head_dim].reshape(share_rows, total_width)
    gate_rows = ordered[:, :, head_dim:qu_cols].reshape(share_rows, total_width)
    x_rows = ordered[:, :, qu_cols:].reshape(share_rows, model_width)
    mean_value = jnp.mean(att_rows, axis=1, keepdims=True)
    variance = jnp.mean(att_rows * att_rows, axis=1, keepdims=True) - mean_value * mean_value
    hidden = (
        (att_rows - mean_value) * lax.rsqrt(variance + norm_eps) * norm_gain[None, :] * gate_rows
    ).astype(jnp.bfloat16)
    my_rows = x_rows + jnp.dot(hidden, w_out, preferred_element_type=jnp.float32)
    return my_rows.astype(jnp.bfloat16)


def solution(mesh):
    in_specs = (
        P(("groups", "rank"), None),
        P(("groups", "rank"), None, None, None),
        P(),
        P(),
        P(),
        P("groups", None),
        P(),
        P("groups"),
        P("groups", None),
    )
    out_specs = P(("groups", "rank"), None)
    return jax.shard_map(body, mesh=mesh, in_specs=in_specs, out_specs=out_specs, check_vma=False)
```

profile of v0, /device:TPU:0, one launch (start us, length us, event | category | flops | bytes accessed | tf_op | source)
XLA Modules:
  0.0 151.2 jit_solution(3385824127241586557)
XLA Ops:
  0.0 1.0 fusion.26
  1.0 0.8 fusion.16
  1.8 0.8 select_reduce_fusion
  2.8 0.8 fusion.18
  3.8 1.6 %gather_fusion.1 = bf16[4,4,64,256]{3,2,1,0:T(8,128)(2,1)S(1)} fusion(bf16[4,4,64,256]{3,2,1,0:T(8,128)(2,1)} %param.11, s32[1024]{0:T(1024)S(1)} %pad_clamp_fusion.1), kind=kCustom, calls=%fused_computation.1 | custom fusion | bytes 1048592 | tf_op jit(solution)/shard_map/jit(_take)/gather | solution.py:66
  5.4 1.0 fusion.6
  6.4 7.4 %all-to-all-start = ((bf16[16,64,256]{2,1,0:T(8,128)(2,1)}), bf16[16,64,256]{2,1,0:T(8,128)(2,1)}, u32[]{:S(2)}, u32[]{:S(2)}) async-start(bf16[16,64,256]{2,1,0:T(8,128)(2,1)} %fusion.6), calls=%async_computation | async-start | bytes 1048576 | tf_op jit(solution)/shard_map/all_to_all | solution.py:69
  13.8 0.6 fusion.22
  16.4 0.8 compare_select_fusion
  17.2 23.5 %all_gather.3 = bf16[256,1024]{1,0:T(8,128)(2,1)S(1)} all-gather(bf16[16,1024]{1,0:T(8,128)(2,1)} %param.10), channel_id=1, replica_groups=mesh['groups'=2,'rank'=16] {'rank'}, dimensions={0}, use_global_device_ids=true | all-gather | bytes 557056 | tf_op jit(solution)/shard_map/all_gather | solution.py:71
  40.7 9.7 %gather_fusion = bf16[2048,1024]{1,0:T(8,128)(2,1)} fusion(bf16[256,1024]{1,0:T(8,128)(2,1)S(1)} %all_gather.3, s32[2048]{0:T(1024)S(1)} %broadcast_clamp_fusion), kind=kCustom, calls=%fused_computation | custom fusion | bytes 8396800 | tf_op jit(solution)/shard_map/jit(_take)/gather | solution.py:72
  50.3 3.8 %broadcast_select_fusion = bf16[2048,1024]{1,0:T(8,128)(2,1)} fusion(bf16[2048,1024]{1,0:T(8,128)(2,1)} %gather_fusion, pred[2048]{0:T(1024)(128)(4,1)S(1)} %compare_and_fusion), kind=kLoop, calls=%fused_computation.7 | loop fusion | flops 2097152 | bytes 8390656 | tf_op jit(solution)/shard_map/jit(_take)/select_n | solution.py:72
  54.1 4.8 %multiply_convert_fusion.1 = bf16[2048,256]{0,1:T(8,128)(2,1)} fusion(bf16[2048,1024]{1,0:T(8,128)(2,1)} %broadcast_select_fusion, bf16[1024,1024]{1,0:T(8,128)(2,1)S(1)} %copy-done, s32[]{:T(128)S(6)} %select_n.171), kind=kOutput, calls=%fused_computation.11 | convolution fusion | flops 1076363264 | bytes 5767172 | tf_op jit(solution)/shard_map/dot_general | solution.py:74
  58.9 1.1 slice_convert_fusion
  60.0 1.3 copy.32
  61.4 2.7 %dynamic-slice_convert_fusion = f32[2048,256]{1,0:T(8,128)} fusion(bf16[2048,1024]{1,0:T(8,128)(2,1)} %broadcast_select_fusion, s32[]{:T(128)S(6)} %select_n.171), kind=kLoop, calls=%fused_computation.22 | loop fusion | flops 524288 | bytes 3145732 | tf_op jit(solution)/shard_map/convert_element_type | solution.py:86
  64.1 4.8 %fusion = f32[2048,128]{1,0:T(8,128)} fusion(bf16[2048,256]{0,1:T(8,128)(2,1)} %multiply_convert_fusion.1, bf16[1024,256]{1,0:T(8,128)(2,1)} %bitcast.6), kind=kOutput, calls=%fused_computation.15 | convolution fusion | flops 1086324736 | bytes 2097152 | tf_op jit(solution)/shard_map/while/body/eval_jaxpr/cond/branch_1_fun/dot_general | solution.py:27
  68.9 2.3 %pad_maximum_fusion = f32[2048,512]{1,0:T(8,128)S(1)} fusion(f32[2048,256]{1,0:T(8,128)} %dynamic-slice_convert_fusion, f32[2048,128]{1,0:T(8,128)S(1)} %copy-done.4, f32[2048,128]{1,0:T(8,128)} %fusion), kind=kLoop, calls=%fused_computation.4 | loop fusion | flops 2097152 | bytes 8388608 | tf_op jit(solution)/shard_map/concatenate | solution.py:85
  71.2 2.4 %slice_select_fusion.2 = (f32[1024,512]{1,0:T(8,128)}, f32[1024,512]{1,0:T(8,128)}) fusion(f32[2048,512]{1,0:T(8,128)S(1)} %pad_maximum_fusion, pred[]{:T(512)S(6)} %eq.36), kind=kLoop, calls=%fused_computation.14 | loop fusion | flops 1048576 | bytes 8388609 | tf_op jit(solution)/shard_map/jit(_where)/select_n | solution.py:95
  73.6 1.4 collective-permute-start
  75.0 46.8 %collective-permute-done = f32[2,512,1,512]{3,1,2,0:T(8,128)} collective-permute-done((f32[2,512,1,512]{3,1,2,0:T(8,128)}, f32[2,512,1,512]{3,1,2,0:T(8,128)}, u32[]{:S(2)}, u32[]{:S(2)}) %collective-permute-start) | collective-permute-done | bytes 2097184 | tf_op jit(solution)/shard_map/ppermute | solution.py:11
  121.8 4.5 %maximum_select_fusion = f32[2,512,2,512]{3,1,2,0:T(8,128)S(1)} fusion(f32[2,512,1,512]{3,1,2,0:T(8,128)} %bitcast.45, f32[2,512,1,512]{3,1,2,0:T(8,128)} %collective-permute-done, pred[]{:T(512)S(6)} %eq.36), kind=kLoop, calls=%fused_computation.5 | loop fusion | flops 3145728 | bytes 8388609 | tf_op jit(solution)/shard_map/jit(_where)/select_n | solution.py:97
  126.4 0.5 slice_select_fusion
  127.0 4.1 %collective-permute-done.1 = f32[1,512,2,512]{3,1,2,0:T(8,128)S(1)} collective-permute-done((f32[1,512,2,512]{3,1,2,0:T(8,128)S(1)}, f32[1,512,2,512]{3,1,2,0:T(8,128)S(1)}, u32[]{:S(2)}, u32[]{:S(2)}) %collective-permute-start.1) | collective-permute-done | bytes 2097184 | tf_op jit(solution)/shard_map/ppermute | solution.py:11
  131.1 2.5 %maximum_select_fusion.1 = f32[512,4,512]{2,0,1:T(8,128)} fusion(f32[512,2,512]{2,0,1:T(8,128)S(1)} %get-tuple-element.37, f32[512,2,512]{2,0,1:T(8,128)S(1)} %bitcast.46, pred[]{:T(512)S(6)} %eq.35), kind=kLoop, calls=%fused_computation.6 | loop fusion | flops 3145728 | bytes 8388609 | tf_op jit(solution)/shard_map/jit(_where)/select_n | solution.py:97
  133.5 5.0 %gather_fusion.2 = f32[4,512,512]{2,1,0:T(8,128)} fusion(f32[512,4,512]{2,0,1:T(8,128)} %maximum_select_fusion.1, s32[1024]{0:T(1024)S(1)} %pad_clamp_fusion), kind=kCustom, calls=%fused_computation.2 | custom fusion | bytes 8388624 | tf_op jit(solution)/shard_map/gather | solution.py:106
  138.5 2.8 %slice_reduce_fusion = (f32[512]{0:T(512)S(1)}, f32[512]{0:T(512)S(1)}, f32[512,4,128]{2,0,1:T(8,128)}, f32[512,4,128]{2,0,1:T(8,128)S(1)}) fusion(f32[512,4,512]{2,0,1:T(8,128)} %bitcast.42), kind=kLoop, calls=%fused_computation.67 | loop fusion | flops 785408 | bytes 4198400 | tf_op jit(solution)/shard_map/reduce_sum | solution.py:110
  141.6 1.6 %slice_bitcast_fusion = f32[4,64,8,256]{3,2,1,0:T(8,128)} fusion(f32[512,4,512]{2,0,1:T(8,128)S(1)} %bitcast.43), kind=kLoop, calls=%fused_computation.8 | loop fusion | bytes 4194304
  143.2 2.6 %copy.37 = f32[512,4,128]{0,2,1:T(8,128)} copy(f32[512,4,128]{2,0,1:T(8,128)} %get-tuple-element.34) | data formatting | bytes 2097152 | tf_op jit(solution)/shard_map/slice | solution.py:107
  145.7 1.3 copy.38
  147.0 2.0 %copy.40 = f32[4,64,8,256]{3,2,0,1:T(8,128)S(1)} copy(f32[4,64,8,256]{3,2,1,0:T(8,128)} %slice_bitcast_fusion) | data formatting | bytes 4194304 | tf_op jit(solution)/shard_map/reshape | solution.py:109
  149.5 1.7 %add_convert_fusion = bf16[512,1024]{1,0:T(8,128)(2,1)} fusion(f32[512,1024]{1,0:T(8,128)S(1)} %bitcast.44, bf16[512,512]{0,1:T(8,128)(2,1)S(1)} %fusion.1, bf16[512,1024]{1,0:T(8,128)(2,1)S(1)} %copy-done.5), kind=kOutput, calls=%fused_computation.9 | convolution fusion | flops 537919488 | bytes 4718592 | tf_op jit(solution)/shard_map/dot_general | solution.py:115
  (30 shorter events, 1.2 us)
Async XLA Ops:
  0.0 54.1 %copy-start = (bf16[1024,1024]{1,0:T(8,128)(2,1)S(1)}, bf16[1024,1024]{1,0:T(8,128)(2,1)}, u32[]{:S(2)}) copy-start(bf16[1024,1024]{1,0:T(8,128)(2,1)} %param.12) | copy-start | bytes 6291460
  6.4 57.7 %all-to-all-start = ((bf16[16,64,256]{2,1,0:T(8,128)(2,1)}), bf16[16,64,256]{2,1,0:T(8,128)(2,1)}, u32[]{:S(2)}, u32[]{:S(2)}) async-start(bf16[16,64,256]{2,1,0:T(8,128)(2,1)} %fusion.6), calls=%async_computation | async-start | bytes 1048576 | tf_op jit(solution)/shard_map/all_to_all | solution.py:69
  64.1 4.8 %copy-start.4 = (f32[2048,128]{1,0:T(8,128)S(1)}, f32[2048,128]{1,0:T(8,128)}, u32[]{:S(2)}) copy-start(f32[2048,128]{1,0:T(8,128)} %copy.32) | copy-start | bytes 3145732
  73.6 48.2 %collective-permute-start = (f32[2,512,1,512]{3,1,2,0:T(8,128)}, f32[2,512,1,512]{3,1,2,0:T(8,128)}, u32[]{:S(2)}, u32[]{:S(2)}) collective-permute-start(f32[2,512,1,512]{3,1,2,0:T(8,128)} %bitcast.8), channel_id=1, source_target_pairs={{0,2},{1,3},{2,0},{3,1},{4,6},{5,7},{6,4},{7,5},{8,10},{9,11},{10,... | collective-permute-start | bytes 6291464 | tf_op jit(solution)/shard_map/ppermute | solution.py:11
  126.3 0.7 copy-start.7
  126.9 4.2 %collective-permute-start.1 = (f32[1,512,2,512]{3,1,2,0:T(8,128)S(1)}, f32[1,512,2,512]{3,1,2,0:T(8,128)S(1)}, u32[]{:S(2)}, u32[]{:S(2)}) collective-permute-start(f32[1,512,2,512]{3,1,2,0:T(8,128)S(1)} %get-tuple-element.36), channel_id=1, source_target_pairs={{0,1},{1,0},{2,3},{3,2},{4,5},{5,4},{6,7},{7,6},{8,9},{9,8},{10,11... | collective-permute-start | bytes 6291464 | tf_op jit(solution)/shard_map/ppermute | solution.py:11
  138.5 3.0 %copy-start.1 = (f32[4,512,512]{2,1,0:T(8,128)S(1)}, f32[4,512,512]{2,1,0:T(8,128)}, u32[]{:S(2)}) copy-start(f32[4,512,512]{2,1,0:T(8,128)} %gather_fusion.2) | copy-start | bytes 12582916
  143.2 5.9 %copy-start.6 = (f32[512]{0:T(512)S(1)}, f32[512]{0:T(512)}, u32[]{:S(2)}) copy-start(f32[512]{0:T(512)} %param.14) | copy-start | bytes 6148
  147.0 2.0 %copy-start.2 = (f32[512,4,128]{0,2,1:T(8,128)S(1)}, f32[512,4,128]{0,2,1:T(8,128)}, u32[]{:S(2)}) copy-start(f32[512,4,128]{0,2,1:T(8,128)} %copy.37) | copy-start | bytes 3145732
  147.0 2.2 %copy-start.3 = (f32[512,4,128]{0,2,1:T(8,128)S(1)}, f32[512,4,128]{0,2,1:T(8,128)}, u32[]{:S(2)}) copy-start(f32[512,4,128]{0,2,1:T(8,128)} %copy.38) | copy-start | bytes 3145732
  147.0 2.5 %copy-start.5 = (bf16[512,1024]{1,0:T(8,128)(2,1)S(1)}, bf16[512,1024]{1,0:T(8,128)(2,1)}, u32[]{:S(2)}) copy-start(bf16[512,1024]{1,0:T(8,128)(2,1)} %param.13) | copy-start | bytes 3145732
where the time goes:
time: 152 us; the launch traced here: 151 us
  waiting for transfers between devices  50.9 us (33%)
  other arithmetic  28.6 us (19%)
  local copies, waits for them, and re-layouts  25.9 us (17%)
  blocking collectives  23.5 us (15%)
  matrix products  11.3 us (7%)
  starting transfers between devices  8.88 us (6%)
  between operations  2.11 us (1%)
    ppermute x2, waiting for transfers between devices, partner(): lax.ppermute(shard, axis, [(i, i ^ 1 << bit) for i in range(lax.axis_size...  50.9 us
    all_gather x1, blocking collectives, body(): whole_pool = lax.all_gather(pool, 'rank', axis=0, tiled=True)  23.5 us
    gather x1, local copies, waits for them, and re-layouts, body(): cand_rows = jnp.take(whole_pool, my_ids, axis=0)  9.66 us
    all_to_all x1, starting transfers between devices, body(): lax.all_to_all(outgoing, 'rank', split_axis=0, concat_axis=0, tiled=True)  7.44 us
    select_n x2, other arithmetic, body(): jnp.where(upper_side, jnp.concatenate([received, keeping], axis=2), jnp.c...  6.96 us
    gather x1, local copies, waits for them, and re-layouts, body(): ordered = state[0][:, jnp.array(reversal, dtype=jnp.int32), :]  4.97 us
    dot_general x1, matrix products, compute(): jnp.dot(weights, value_part, preferred_element_type=jnp.float32)  4.83 us
    dot_general x1, matrix products, body(): jnp.dot(cand_rows, w_head, preferred_element_type=jnp.float32)  4.77 us
  transfers between devices with their start and end apart: 3, of which 2 were waited for; matrix products, arithmetic and copies ran while one was open for 16% of the time, Pallas kernels for 0%

commit v1 on v0

--- a/solution.py
+++ b/solution.py
@@ -68,7 +68,8 @@
     outgoing = outgoing.reshape(devices, block_len, pair_width)
     incoming = lax.all_to_all(outgoing, "rank", split_axis=0, concat_axis=0, tiled=True)
     my_ids = lax.dynamic_index_in_dim(cand_ids, my_user, 0, keepdims=False)
-    whole_pool = lax.all_gather(pool, "rank", axis=0, tiled=True)
+    copies = jnp.concatenate([pool] * lax.axis_size("rank"), axis=0)
+    whole_pool = lax.all_to_all(copies, "rank", 0, 0, tiled=True)
     cand_rows = jnp.take(whole_pool, my_ids, axis=0)
     w_head = lax.dynamic_slice_in_dim(w_qu, my_head * qu_cols, qu_cols, 1)
     head_qu = jax.nn.silu(jnp.dot(cand_rows, w_head, preferred_element_type=jnp.float32)).astype(

time: 152 us -> 155 us (1.020)
  blocking collectives: 23.5 us -> 0 us
  local copies, waits for them, and re-layouts: 25.9 us -> 49 us
  starting transfers between devices: 8.88 us -> 13.6 us
  waiting for transfers between devices: 50.9 us -> 54.8 us
  matrix products: 11.3 us -> 8.05 us
  other arithmetic: 28.6 us -> 25.4 us
    all_gather x1 -> x0, blocking collectives: 23.5 us -> none  [body(): whole_pool = lax.all_gather(pool, 'rank', axis=0, tiled=True)]
    unnamed x17 -> x32, local copies, waits for them, and re-layouts: 2.16 us -> 23.9 us
    all_to_all x0 -> x1, starting transfers between devices: none -> 7.39 us  [body(): whole_pool = lax.all_to_all(copies, 'rank', 0, 0, tiled=True)]
    all_to_all x0 -> x1, waiting for transfers between devices: none -> 4.39 us  [body(): whole_pool = lax.all_to_all(copies, 'rank', 0, 0, tiled=True)]
    all_to_all x1, starting transfers between devices: 7.44 us -> 4.24 us  [body(): lax.all_to_all(outgoing, 'rank', split_axis=0, concat_axis=0, tiled=True)]
    dot_general x1, matrix products: 4.77 us -> 1.6 us  [body(): jnp.dot(cand_rows, w_head, preferred_element_type=jnp.float32)]
  transfers between devices with their start and end apart: 3 -> 4, of which waited for: 2 -> 3; matrix products, arithmetic and copies ran while one was open for 16% -> 15% of each run, Pallas kernels for 0% -> 0%
where the time goes in v1:
time: 155 us; the launch traced here: 153 us
  waiting for transfers between devices  54.8 us (35%)
  local copies, waits for them, and re-layouts  49 us (32%)
  other arithmetic  25.4 us (16%)
  starting transfers between devices  13.6 us (9%)
  matrix products  8.05 us (5%)
  between operations  2.32 us (1%)
    ppermute x2, waiting for transfers between devices, partner(): lax.ppermute(shard, axis, [(i, i ^ 1 << bit) for i in range(lax.axis_size...  50.4 us
    unnamed x32, local copies, waits for them, and re-layouts  23.9 us
    gather x1, local copies, waits for them, and re-layouts, body(): cand_rows = jnp.take(whole_pool, my_ids, axis=0)  9.67 us
    all_to_all x1, starting transfers between devices, body(): whole_pool = lax.all_to_all(copies, 'rank', 0, 0, tiled=True)  7.39 us
    select_n x2, other arithmetic, body(): jnp.where(upper_side, jnp.concatenate([received, keeping], axis=2), jnp.c...  6.96 us
    gather x1, local copies, waits for them, and re-layouts, body(): ordered = state[0][:, jnp.array(reversal, dtype=jnp.int32), :]  4.97 us
    dot_general x1, matrix products, compute(): jnp.dot(weights, value_part, preferred_element_type=jnp.float32)  4.74 us
    all_to_all x1, waiting for transfers between devices, body(): whole_pool = lax.all_to_all(copies, 'rank', 0, 0, tiled=True)  4.39 us
  transfers between devices with their start and end apart: 4, of which 3 were waited for; matrix products, arithmetic and copies ran while one was open for 15% of the time, Pallas kernels for 0%

profile of v1, /device:TPU:0, one launch (start us, length us, event | category | flops | bytes accessed | tf_op | source)
XLA Modules:
  0.0 153.2 jit_solution(2008306571835859848)
XLA Ops:
  0.0 1.5 constant_dynamic-update-slice_fusion.15
  1.5 1.4 constant_dynamic-update-slice_fusion.14
  2.9 1.4 constant_dynamic-update-slice_fusion.13
  4.3 1.4 constant_dynamic-update-slice_fusion.12
  5.6 1.4 constant_dynamic-update-slice_fusion.11
  7.0 1.4 constant_dynamic-update-slice_fusion.10
  8.4 1.4 constant_dynamic-update-slice_fusion.9
  9.8 1.4 constant_dynamic-update-slice_fusion.8
  11.1 1.4 constant_dynamic-update-slice_fusion.7
  12.5 1.4 constant_dynamic-update-slice_fusion.6
  22.1 7.4 %all-to-all-start = ((bf16[16,16,1024]{2,1,0:T(8,128)(2,1)}), bf16[16,16,1024]{2,1,0:T(8,128)(2,1)S(1)}, u32[]{:S(2)}, u32[]{:S(2)}) async-start(bf16[16,16,1024]{2,1,0:T(8,128)(2,1)} %bitcast.1), calls=%async_computation | async-start | bytes 1048576 | tf_op jit(solution)/shard_map/all_to_all | solution.py:72
  36.0 1.6 %gather_fusion.1 = bf16[4,4,64,256]{3,2,1,0:T(8,128)(2,1)S(1)} fusion(bf16[4,4,64,256]{3,2,1,0:T(8,128)(2,1)} %param.11, s32[1024]{0:T(1024)S(1)} %pad_clamp_fusion.1), kind=kCustom, calls=%fused_computation.1 | custom fusion | bytes 1048592 | tf_op jit(solution)/shard_map/jit(_take)/gather | solution.py:66
  39.4 4.4 %all-to-all-done = bf16[16,16,1024]{2,1,0:T(8,128)(2,1)S(1)} async-done(((bf16[16,16,1024]{2,1,0:T(8,128)(2,1)}), bf16[16,16,1024]{2,1,0:T(8,128)(2,1)S(1)}, u32[]{:S(2)}, u32[]{:S(2)}) %all-to-all-start) | async-done | bytes 524320 | tf_op jit(solution)/shard_map/all_to_all | solution.py:72
  43.8 4.2 %all-to-all-start.1 = ((bf16[16,64,256]{2,1,0:T(8,128)(2,1)}), bf16[16,64,256]{2,1,0:T(8,128)(2,1)}, u32[]{:S(2)}, u32[]{:S(2)}) async-start(bf16[16,64,256]{2,1,0:T(8,128)(2,1)} %fusion.6), calls=%async_computation.1 | async-start | bytes 1048576 | tf_op jit(solution)/shard_map/all_to_all | solution.py:69
  48.1 9.7 %gather_fusion = bf16[2048,1024]{1,0:T(8,128)(2,1)} fusion(bf16[256,1024]{1,0:T(8,128)(2,1)S(1)} %bitcast.44, s32[2048]{0:T(1024)S(1)} %broadcast_clamp_fusion), kind=kCustom, calls=%fused_computation | custom fusion | bytes 8396800 | tf_op jit(solution)/shard_map/jit(_take)/gather | solution.py:73
  57.7 2.5 %broadcast_select_fusion = bf16[2048,1024]{1,0:T(8,128)(2,1)S(1)} fusion(bf16[2048,1024]{1,0:T(8,128)(2,1)} %gather_fusion, pred[2048]{0:T(1024)(128)(4,1)S(1)} %compare_and_fusion), kind=kLoop, calls=%fused_computation.7 | loop fusion | flops 2097152 | bytes 8390656 | tf_op jit(solution)/shard_map/jit(_take)/select_n | solution.py:73
  60.2 1.6 %dynamic-slice_convert_fusion = f32[2048,256]{1,0:T(8,128)} fusion(bf16[2048,1024]{1,0:T(8,128)(2,1)S(1)} %broadcast_select_fusion, s32[]{:T(128)S(6)} %select_n.171), kind=kLoop, calls=%fused_computation.22 | loop fusion | flops 524288 | bytes 3145732 | tf_op jit(solution)/shard_map/convert_element_type | solution.py:87
  61.8 1.6 %multiply_convert_fusion.1 = bf16[2048,256]{0,1:T(8,128)(2,1)S(1)} fusion(bf16[2048,1024]{1,0:T(8,128)(2,1)S(1)} %broadcast_select_fusion, bf16[1024,1024]{1,0:T(8,128)(2,1)S(1)} %copy-done, s32[]{:T(128)S(6)} %select_n.171), kind=kOutput, calls=%fused_computation.11 | convolution fusion | flops 1076363264 | bytes 5767172 | tf_op jit(solution)/shard_map/dot_general | solution.py:75
  64.5 4.7 %fusion = f32[2048,128]{1,0:T(8,128)} fusion(bf16[2048,256]{0,1:T(8,128)(2,1)} %copy-done.5, bf16[1024,256]{1,0:T(8,128)(2,1)} %bitcast.8), kind=kOutput, calls=%fused_computation.15 | convolution fusion | flops 1086324736 | bytes 2097152 | tf_op jit(solution)/shard_map/while/body/eval_jaxpr/cond/branch_1_fun/dot_general | solution.py:27
  70.6 2.6 %pad_maximum_fusion = f32[2048,512]{1,0:T(8,128)S(1)} fusion(f32[2048,256]{1,0:T(8,128)} %dynamic-slice_convert_fusion, f32[2048,128]{1,0:T(8,128)} %copy.32, f32[2048,128]{1,0:T(8,128)} %fusion), kind=kLoop, calls=%fused_computation.4 | loop fusion | flops 2097152 | bytes 8388608 | tf_op jit(solution)/shard_map/concatenate | solution.py:86
  73.1 2.4 %slice_select_fusion.2 = (f32[1024,512]{1,0:T(8,128)}, f32[1024,512]{1,0:T(8,128)}) fusion(f32[2048,512]{1,0:T(8,128)S(1)} %pad_maximum_fusion, pred[]{:T(512)S(6)} %eq.36), kind=kLoop, calls=%fused_computation.14 | loop fusion | flops 1048576 | bytes 8388609 | tf_op jit(solution)/shard_map/jit(_where)/select_n | solution.py:96
  75.6 1.9 %collective-permute-start = (f32[2,512,1,512]{3,1,2,0:T(8,128)}, f32[2,512,1,512]{3,1,2,0:T(8,128)}, u32[]{:S(2)}, u32[]{:S(2)}) collective-permute-start(f32[2,512,1,512]{3,1,2,0:T(8,128)} %bitcast.10), channel_id=1, source_target_pairs={{0,2},{1,3},{2,0},{3,1},{4,6},{5,7},{6,4},{7,5},{8,10},{9,11},{10,... | collective-permute-start | bytes 6291464 | tf_op jit(solution)/shard_map/ppermute | solution.py:11
  77.5 46.3 %collective-permute-done = f32[2,512,1,512]{3,1,2,0:T(8,128)} collective-permute-done((f32[2,512,1,512]{3,1,2,0:T(8,128)}, f32[2,512,1,512]{3,1,2,0:T(8,128)}, u32[]{:S(2)}, u32[]{:S(2)}) %collective-permute-start) | collective-permute-done | bytes 2097184 | tf_op jit(solution)/shard_map/ppermute | solution.py:11
  123.8 4.5 %maximum_select_fusion = f32[2,512,2,512]{3,1,2,0:T(8,128)S(1)} fusion(f32[2,512,1,512]{3,1,2,0:T(8,128)} %bitcast.48, f32[2,512,1,512]{3,1,2,0:T(8,128)} %collective-permute-done, pred[]{:T(512)S(6)} %eq.36), kind=kLoop, calls=%fused_computation.5 | loop fusion | flops 3145728 | bytes 8388609 | tf_op jit(solution)/shard_map/jit(_where)/select_n | solution.py:98
  129.0 4.1 %collective-permute-done.1 = f32[1,512,2,512]{3,1,2,0:T(8,128)S(1)} collective-permute-done((f32[1,512,2,512]{3,1,2,0:T(8,128)S(1)}, f32[1,512,2,512]{3,1,2,0:T(8,128)S(1)}, u32[]{:S(2)}, u32[]{:S(2)}) %collective-permute-start.1) | collective-permute-done | bytes 2097184 | tf_op jit(solution)/shard_map/ppermute | solution.py:11
  133.1 2.5 %maximum_select_fusion.1 = f32[512,4,512]{2,0,1:T(8,128)} fusion(f32[512,2,512]{2,0,1:T(8,128)S(1)} %get-tuple-element.37, f32[512,2,512]{2,0,1:T(8,128)S(1)} %bitcast.49, pred[]{:T(512)S(6)} %eq.35), kind=kLoop, calls=%fused_computation.6 | loop fusion | flops 3145728 | bytes 8388609 | tf_op jit(solution)/shard_map/jit(_where)/select_n | solution.py:98
  135.5 5.0 %gather_fusion.2 = f32[4,512,512]{2,1,0:T(8,128)} fusion(f32[512,4,512]{2,0,1:T(8,128)} %maximum_select_fusion.1, s32[1024]{0:T(1024)S(1)} %pad_clamp_fusion), kind=kCustom, calls=%fused_computation.2 | custom fusion | bytes 8388624 | tf_op jit(solution)/shard_map/gather | solution.py:107
  140.5 2.8 %slice_reduce_fusion = (f32[512]{0:T(512)S(1)}, f32[512]{0:T(512)S(1)}, f32[512,4,128]{2,0,1:T(8,128)}, f32[512,4,128]{2,0,1:T(8,128)S(1)}) fusion(f32[512,4,512]{2,0,1:T(8,128)} %bitcast.45), kind=kLoop, calls=%fused_computation.83 | loop fusion | flops 785408 | bytes 4198400 | tf_op jit(solution)/shard_map/reduce_sum | solution.py:111
  143.5 1.6 %slice_bitcast_fusion = f32[4,64,8,256]{3,2,1,0:T(8,128)} fusion(f32[512,4,512]{2,0,1:T(8,128)S(1)} %bitcast.46), kind=kLoop, calls=%fused_computation.8 | loop fusion | bytes 4194304
  145.1 2.6 %copy.37 = f32[512,4,128]{0,2,1:T(8,128)} copy(f32[512,4,128]{2,0,1:T(8,128)} %get-tuple-element.34) | data formatting | bytes 2097152 | tf_op jit(solution)/shard_map/slice | solution.py:108
  149.0 2.0 %copy.40 = f32[4,64,8,256]{3,2,0,1:T(8,128)S(1)} copy(f32[4,64,8,256]{3,2,1,0:T(8,128)} %slice_bitcast_fusion) | data formatting | bytes 4194304 | tf_op jit(solution)/shard_map/reshape | solution.py:110
  151.5 1.7 %add_convert_fusion = bf16[512,1024]{1,0:T(8,128)(2,1)} fusion(f32[512,1024]{1,0:T(8,128)S(1)} %bitcast.47, bf16[512,512]{0,1:T(8,128)(2,1)S(1)} %fusion.1, bf16[512,1024]{1,0:T(8,128)(2,1)S(1)} %copy-done.4), kind=kOutput, calls=%fused_computation.9 | convolution fusion | flops 537919488 | bytes 4718592 | tf_op jit(solution)/shard_map/dot_general | solution.py:116
  (47 shorter events, 19.3 us)
Async XLA Ops:
  0.0 61.8 %copy-start = (bf16[1024,1024]{1,0:T(8,128)(2,1)S(1)}, bf16[1024,1024]{1,0:T(8,128)(2,1)}, u32[]{:S(2)}) copy-start(bf16[1024,1024]{1,0:T(8,128)(2,1)} %param.12) | copy-start | bytes 6291460
  22.1 21.7 %all-to-all-start = ((bf16[16,16,1024]{2,1,0:T(8,128)(2,1)}), bf16[16,16,1024]{2,1,0:T(8,128)(2,1)S(1)}, u32[]{:S(2)}, u32[]{:S(2)}) async-start(bf16[16,16,1024]{2,1,0:T(8,128)(2,1)} %bitcast.1), calls=%async_computation | async-start | bytes 1048576 | tf_op jit(solution)/shard_map/all_to_all | solution.py:72
  43.8 20.7 %all-to-all-start.1 = ((bf16[16,64,256]{2,1,0:T(8,128)(2,1)}), bf16[16,64,256]{2,1,0:T(8,128)(2,1)}, u32[]{:S(2)}, u32[]{:S(2)}) async-start(bf16[16,64,256]{2,1,0:T(8,128)(2,1)} %fusion.6), calls=%async_computation.1 | async-start | bytes 1048576 | tf_op jit(solution)/shard_map/all_to_all | solution.py:69
  63.4 1.0 copy-start.5
  75.6 48.2 %collective-permute-start = (f32[2,512,1,512]{3,1,2,0:T(8,128)}, f32[2,512,1,512]{3,1,2,0:T(8,128)}, u32[]{:S(2)}, u32[]{:S(2)}) collective-permute-start(f32[2,512,1,512]{3,1,2,0:T(8,128)} %bitcast.10), channel_id=1, source_target_pairs={{0,2},{1,3},{2,0},{3,1},{4,6},{5,7},{6,4},{7,5},{8,10},{9,11},{10,... | collective-permute-start | bytes 6291464 | tf_op jit(solution)/shard_map/ppermute | solution.py:11
  128.3 0.7 copy-start.7
  128.8 4.2 %collective-permute-start.1 = (f32[1,512,2,512]{3,1,2,0:T(8,128)S(1)}, f32[1,512,2,512]{3,1,2,0:T(8,128)S(1)}, u32[]{:S(2)}, u32[]{:S(2)}) collective-permute-start(f32[1,512,2,512]{3,1,2,0:T(8,128)S(1)} %get-tuple-element.36), channel_id=1, source_target_pairs={{0,1},{1,0},{2,3},{3,2},{4,5},{5,4},{6,7},{7,6},{8,9},{9,8},{10,11... | collective-permute-start | bytes 6291464 | tf_op jit(solution)/shard_map/ppermute | solution.py:11
  140.5 3.0 %copy-start.1 = (f32[4,512,512]{2,1,0:T(8,128)S(1)}, f32[4,512,512]{2,1,0:T(8,128)}, u32[]{:S(2)}) copy-start(f32[4,512,512]{2,1,0:T(8,128)} %gather_fusion.2) | copy-start | bytes 12582916
  145.1 5.9 %copy-start.6 = (f32[512]{0:T(512)S(1)}, f32[512]{0:T(512)}, u32[]{:S(2)}) copy-start(f32[512]{0:T(512)} %param.14) | copy-start | bytes 6148
  149.0 2.0 %copy-start.2 = (f32[512,4,128]{0,2,1:T(8,128)S(1)}, f32[512,4,128]{0,2,1:T(8,128)}, u32[]{:S(2)}) copy-start(f32[512,4,128]{0,2,1:T(8,128)} %copy.37) | copy-start | bytes 3145732
  149.0 2.2 %copy-start.3 = (f32[512,4,128]{0,2,1:T(8,128)S(1)}, f32[512,4,128]{0,2,1:T(8,128)}, u32[]{:S(2)}) copy-start(f32[512,4,128]{0,2,1:T(8,128)} %copy.38) | copy-start | bytes 3145732
  149.0 2.5 %copy-start.4 = (bf16[512,1024]{1,0:T(8,128)(2,1)S(1)}, bf16[512,1024]{1,0:T(8,128)(2,1)}, u32[]{:S(2)}) copy-start(bf16[512,1024]{1,0:T(8,128)(2,1)} %param.13) | copy-start | bytes 3145732
